TPU v7x, 32 devices: a whole 2x2x4 slice. The times are simulated.
32 devices in a mesh: groups: 2 (over x), ctx: 8 (over z, y), head: 2 (over core).
Axes of the slice: x: 2, y: 2, z: 4, core: 2. Of those that a mesh axis runs over, the one named last changes fastest.
Arguments:
- queries: bfloat16 [4096, 2048], P(('groups', 'ctx'), 'head'), parts along dimension 0, may hold values from -180 to 180
- keys: bfloat16 [4096, 2048], P(('groups', 'ctx'), 'head'), parts along dimension 0, may hold values from -6 to 6
- values: bfloat16 [4096, 2048], P(('groups', 'ctx'), 'head'), parts along dimension 0, may hold values from -6 to 6
- out_weight: bfloat16 [2048, 2048], P(None, 'head'), may hold values from -0.125 to 0.125
- random_blocks: int32 [32, 3], P('groups'), parts along dimension 0, may hold values from 0 to 15, as said below
- window_blocks: int32 [32], P(('groups', 'ctx')), parts along dimension 0, may hold values from 0 to 1
- global_blocks: int32 [4], P('groups'), parts along dimension 0, may hold values from 0 to 15, as said below
Outputs:
- layer_out: bfloat16 [4096, 2048], P(('groups', 'ctx'), 'head'), parts along dimension 0
There are 2 independent parts, one for each index of `groups`. A program takes and returns all parts, laid end to end along the dimension named above; an argument that names none is the same for every part. Nothing has to cross between parts.
Inputs may be any that keep to these rules, and one draw needn't show every extreme that they name: `random_blocks`: the random blocks named in the rows of one index j of ctx (rows j * 2 to j * 2 + 1) lie outside blocks j * 2 to j * 2 + 1; counted with repeats, at most 1 of them lie in the blocks k * 2 to k * 2 + 1 of any one other index k, and exactly 1 for some k. `global_blocks`: 2 different block numbers.
All inputs are finite; a program needn't handle non-finite values.
Results may differ from a plain program's by a relative error of at most 0.0055.
Values may be sent and summed in bfloat16 or wider, within the bound.
A program may use at most 128 MiB of HBM per device.

v0:
```python
import math
import jax
import jax.numpy as jnp
from jax import lax
from jax.sharding import PartitionSpec as P

HEAD = 128
BLOCK = 128
WMAX = 1
GLOB = 2
RAND = 3
LARGE_NEG = -1e30


def with_halo(block, sides, width):
    for axis, dim in sides:
        count = lax.axis_size(axis)
        forward = [(i, i + 1) for i in range(count - 1)]
        backward = [(target, source) for source, target in forward]
        low = lax.ppermute(
            lax.slice_in_dim(block, block.shape[dim] - width, None, axis=dim), axis, forward
        )
        high = lax.ppermute(lax.slice_in_dim(block, 0, width, axis=dim), axis, backward)
        block = jnp.concatenate([low, block, high], axis=dim)
    return block


def split_heads(tensor):
    return tensor.reshape(tensor.shape[:-1] + (tensor.shape[-1] // HEAD, HEAD))


def block_partial(query_rows, key_rows, value_rows):
    query_heads = split_heads(query_rows)
    key_heads = split_heads(key_rows)
    value_heads = split_heads(value_rows)
    scores = jnp.einsum(
        "gqhd,gckhd->gchqk", query_heads, key_heads, preferred_element_type=jnp.float32
    ) * (1.0 / math.sqrt(HEAD))
    row_peak = jnp.max(scores, axis=-1)
    weights = jnp.exp(scores - row_peak[..., None])
    row_total = jnp.sum(weights, axis=-1)
    partial_out = jnp.einsum(
        "gchqk,gckhd->gcqhd",
        weights.astype(jnp.bfloat16),
        value_heads,
        preferred_element_type=jnp.float32,
    )
    partial_out = partial_out.reshape(partial_out.shape[:-2] + (-1,))
    return (partial_out, jnp.swapaxes(row_peak, -1, -2), jnp.swapaxes(row_total, -1, -2))


def combine(partial_out, row_peak, row_total, used_flags):
    used_mask = used_flags[:, :, None, None]
    best_peak = jnp.max(jnp.where(used_mask, row_peak, LARGE_NEG), axis=1, keepdims=True)
    factor = jnp.where(used_mask, jnp.exp(row_peak - best_peak), 0.0)
    weighted = jnp.sum(split_heads(partial_out) * factor[..., None], axis=1)
    normalizer = jnp.sum(row_total * factor, axis=1)
    result = weighted / normalizer[..., None]
    return result.reshape(result.shape[:-2] + (-1,))


def candidates(first_block, block_count, widths, global_ids, random_rows, total_blocks):
    query_ids = first_block + jnp.arange(block_count, dtype=jnp.int32)
    offsets = jnp.arange(-WMAX, WMAX + 1, dtype=jnp.int32)
    window_ids = query_ids[:, None] + offsets[None, :]
    window_valid = (
        (jnp.abs(offsets)[None, :] <= widths[:, None])
        & (window_ids >= 0)
        & (window_ids < total_blocks)
    )
    global_rows = jnp.broadcast_to(global_ids[None, :], (block_count, GLOB))
    block_ids = jnp.concatenate([window_ids, global_rows, random_rows], axis=1)
    valid = jnp.concatenate(
        [window_valid, jnp.ones((block_count, GLOB + RAND), dtype=bool)], axis=1
    )
    width_all = block_ids.shape[1]
    same_block = block_ids[:, :, None] == block_ids[:, None, :]
    earlier = jnp.arange(width_all)[None, :] < jnp.arange(width_all)[:, None]
    shadowed = jnp.any(same_block & valid[:, None, :] & earlier[None, :, :], axis=2)
    return (block_ids, valid & jnp.logical_not(shadowed))


def per_device(queries, keys, values, out_weight, random_blocks, window_blocks, global_blocks):
    ctx_count = lax.axis_size("ctx")
    position = lax.axis_index("ctx")
    tok_rows, row_width = queries.shape
    dev_blocks = tok_rows // BLOCK
    total_blocks = dev_blocks * ctx_count
    requests = dev_blocks * RAND
    capacity = (requests + ctx_count - 2) // (ctx_count - 1)
    first_block = position * dev_blocks
    key_value = jnp.stack([keys, values])
    own_blocks = key_value.reshape(2, dev_blocks, BLOCK, row_width)
    extended = with_halo(key_value, (("ctx", 1),), WMAX * BLOCK)
    rim_blocks = extended.reshape(2, dev_blocks + 2 * WMAX, BLOCK, row_width)
    global_owner = global_blocks // dev_blocks
    global_slot = global_blocks % dev_blocks
    picked = jnp.take(own_blocks, global_slot, axis=1)
    owned_here = (global_owner == position)[None, :, None, None]
    global_terms = jnp.where(owned_here, picked.astype(jnp.float32), 0.0)
    global_pairs = lax.psum(global_terms.astype(jnp.bfloat16), "ctx")
    request_table = random_blocks.reshape(ctx_count, requests)
    owners = request_table // dev_blocks
    within = request_table % dev_blocks
    same_owner = owners[:, :, None] == owners[:, None, :]
    before = jnp.arange(requests)[None, :] < jnp.arange(requests)[:, None]
    rank_table = jnp.sum(same_owner & before[None, :, :], axis=2)
    slot_ids = jnp.arange(capacity, dtype=jnp.int32)
    toward_me = (owners == position)[:, :, None] & (
        rank_table[:, :, None] == slot_ids[None, None, :]
    )
    send_index = jnp.sum(jnp.where(toward_me, within[:, :, None], 0), axis=1)
    my_owner = lax.dynamic_index_in_dim(owners, position, 0, keepdims=False)
    my_rank = lax.dynamic_index_in_dim(rank_table, position, 0, keepdims=False)
    my_slot = my_owner * capacity + my_rank
    my_random = lax.dynamic_slice_in_dim(random_blocks, first_block, dev_blocks, 0)
    block_ids, used_flags = candidates(
        first_block, dev_blocks, window_blocks, global_blocks, my_random, total_blocks
    )
    window_index = (
        jnp.arange(dev_blocks, dtype=jnp.int32)[:, None]
        + WMAX
        + jnp.arange(-WMAX, WMAX + 1, dtype=jnp.int32)[None, :]
    )
    global_index = jnp.broadcast_to(
        dev_blocks + 2 * WMAX + jnp.arange(GLOB, dtype=jnp.int32)[None, :], (dev_blocks, GLOB)
    )
    local_pool = jnp.concatenate([rim_blocks, global_pairs], axis=1)
    query_blocks = queries.reshape(dev_blocks, BLOCK, row_width)
    slot_hits = (my_owner[:, None, None] == jnp.arange(ctx_count)[None, :, None]) & (
        my_rank[:, None, None] == slot_ids[None, None, :]
    )
    query_pick = jnp.sum(
        jnp.where(slot_hits, (jnp.arange(requests) // RAND)[:, None, None], 0), axis=0
    )
    outgoing = jnp.take(query_blocks, query_pick, axis=0)
    arrived = lax.all_to_all(outgoing, "ctx", split_axis=0, concat_axis=0, tiled=True)
    item_rows = arrived.shape[2]
    partners = jnp.take(own_blocks, send_index, axis=1)
    flat_queries = arrived.reshape(ctx_count * capacity, item_rows, row_width)
    part_out, part_peak, part_total = block_partial(flat_queries, partners[0], partners[1])
    back_out = lax.all_to_all(part_out, "ctx", split_axis=0, concat_axis=0, tiled=True)
    back_peak = lax.all_to_all(part_peak, "ctx", split_axis=0, concat_axis=0, tiled=True)
    back_total = lax.all_to_all(part_total, "ctx", split_axis=0, concat_axis=0, tiled=True)
    head_count = back_peak.shape[-1]
    rand_out = back_out.reshape(ctx_count * capacity, BLOCK, row_width)[my_slot].reshape(
        dev_blocks, RAND, BLOCK, row_width
    )
    rand_peak = back_peak.reshape(ctx_count * capacity, BLOCK, head_count)[my_slot].reshape(
        dev_blocks, RAND, BLOCK, head_count
    )
    rand_total = back_total.reshape(ctx_count * capacity, BLOCK, head_count)[my_slot].reshape(
        dev_blocks, RAND, BLOCK, head_count
    )
    pool_index = jnp.concatenate([window_index, global_index], axis=1)
    remote_parts = (rand_out, rand_peak, rand_total)
    group_size = math.gcd(dev_blocks, max(1, 512 // BLOCK))
    steps_count = dev_blocks // group_size

    def regroup(tensor):
        return tensor.reshape((steps_count, group_size) + tensor.shape[1:])

    def attend(inputs):
        query_group, index_group, used_group, extra_group = inputs
        gathered = jnp.take(local_pool, index_group, axis=1)
        part_out, part_peak, part_total = block_partial(query_group, gathered[0], gathered[1])
        part_out = jnp.concatenate([part_out, extra_group[0]], axis=1)
        part_peak = jnp.concatenate([part_peak, extra_group[1]], axis=1)
        part_total = jnp.concatenate([part_total, extra_group[2]], axis=1)
        return combine(part_out, part_peak, part_total, used_group).astype(jnp.bfloat16)

    extra_groups = tuple((regroup(member) for member in remote_parts))
    attended = lax.map(
        attend, (regroup(query_blocks), regroup(pool_index), regroup(used_flags), extra_groups)
    )
    attended = attended.reshape(tok_rows, row_width)
    layer_sum = jnp.dot(
        lax.all_gather(attended, "head", axis=1, tiled=True),
        out_weight,
        preferred_element_type=jnp.float32,
    )
    return layer_sum.astype(jnp.bfloat16)


def solution(mesh):
    placed = (
        P(("groups", "ctx"), "head"),
        P(("groups", "ctx"), "head"),
        P(("groups", "ctx"), "head"),
        P(None, "head"),
        P("groups", None),
        P(("groups", "ctx")),
        P("groups"),
    )
    return jax.shard_map(
        per_device,
        mesh=mesh,
        in_specs=placed,
        out_specs=P(("groups", "ctx"), "head"),
        check_vma=False,
    )
```

profile of v0, /device:TPU:0, one launch (start us, length us, event | category | flops | bytes accessed | tf_op | source)
XLA Modules:
  0.0 301.7 jit_solution(17253878951724094730)
XLA Ops:
  6.6 0.8 copy.186
  7.4 0.1 copy.191
  7.5 0.1 copy.195
  7.6 0.2 convert_reduce_fusion
  7.8 0.2 add_reduce_fusion
  8.0 0.2 compare_reduce_fusion
  8.2 0.1 fusion.37
  8.4 1.7 gather_fusion.3
  10.1 1.6 fusion.18
  11.7 7.3 %all-to-all-start = ((bf16[8,1,128,1024]{3,2,1,0:T(8,128)(2,1)}), bf16[8,1,128,1024]{3,2,1,0:T(8,128)(2,1)}, u32[]{:S(2)}, u32[]{:S(2)}) async-start(bf16[8,1,128,1024]{3,2,1,0:T(8,128)(2,1)} %fusion.18), calls=%async_computation | async-start | bytes 4194304 | tf_op jit(solution)/shard_map/all_to_all | solution.py:137
  19.1 0.1 copy.196
  19.2 0.1 eq.96
  19.2 0.1 fusion.33
  19.4 0.1 reduce_sum.81
  19.4 0.1 reduce_sum.82
  19.6 0.1 pad_maximum_fusion.2
  19.7 2.7 gather_fusion.2
  22.5 2.7 bitcast_select_fusion
  25.1 1.8 fusion.48
  26.9 2.4 copy.198
  29.3 3.0 %copy.197 = bf16[1,8,1,128,1024]{3,4,1,2,0:T(8,128)(2,1)S(1)} copy(bf16[1,8,1,128,1024]{4,3,0,1,2:T(8,128)(2,1)} %get-tuple-element.41) | data formatting | bytes 4194304 | tf_op jit(solution)/shard_map/slice | solution.py:141
  32.4 35.0 %all-to-all-done = bf16[8,1,128,1024]{3,2,1,0:T(8,128)(2,1)} async-done(((bf16[8,1,128,1024]{3,2,1,0:T(8,128)(2,1)}), bf16[8,1,128,1024]{3,2,1,0:T(8,128)(2,1)}, u32[]{:S(2)}, u32[]{:S(2)}) %all-to-all-start) | async-done | bytes 2097184 | tf_op jit(solution)/shard_map/all_to_all | solution.py:137
  67.4 3.9 %copy.200 = bf16[8,1,128,1024]{2,3,0,1:T(8,128)(2,1)} copy(bf16[8,1,128,1024]{3,2,1,0:T(8,128)(2,1)} %all-to-all-done) | data formatting | bytes 4194304 | tf_op jit(solution)/shard_map/all_to_all | solution.py:137
  71.3 5.7 %bitcast_reduce_fusion.1 = (f32[8,8,128]{2,1,0:T(8,128)}, f32[8,8,128,128]{3,2,1,0:T(8,128)}) fusion(bf16[8,128,8,128]{1,3,2,0:T(8,128)(2,1)} %bitcast.118, bf16[8,128,8,128]{1,3,2,0:T(8,128)(2,1)} %bitcast.119), kind=kOutput, calls=%fused_computation.18 | convolution fusion | flops 270524416 | bytes 8421376 | tf_op jit(solution)/shard_map/gqhd,gckhd->gchqk/dot_general | solution.py:36
  77.0 3.6 %all-to-all-start.2 = ((f32[8,1,128,8]{2,3,1,0:T(8,128)}), f32[8,1,128,8]{2,3,1,0:T(8,128)S(1)}, u32[]{:S(2)}, u32[]{:S(2)}) async-start(f32[8,1,128,8]{2,3,1,0:T(8,128)} %bitcast.39), calls=%async_computation.2 | async-start | bytes 65536 | tf_op jit(solution)/shard_map/all_to_all | solution.py:143
  80.6 3.7 %fusion.6 = f32[8,8,128]{2,1,0:T(8,128)} fusion(f32[8,8,128,128]{3,2,1,0:T(8,128)} %get-tuple-element.49, f32[8,8,128]{2,1,0:T(8,128)} %get-tuple-element.48), kind=kLoop, calls=%fused_computation.20 | loop fusion | flops 3137536 | bytes 4259840 | tf_op jit(solution)/shard_map/reduce_sum | solution.py:41
  84.3 3.0 %all-to-all-done.2 = f32[8,1,128,8]{2,3,1,0:T(8,128)S(1)} async-done(((f32[8,1,128,8]{2,3,1,0:T(8,128)}), f32[8,1,128,8]{2,3,1,0:T(8,128)S(1)}, u32[]{:S(2)}, u32[]{:S(2)}) %all-to-all-start.2) | async-done | bytes 32800 | tf_op jit(solution)/shard_map/all_to_all | solution.py:143
  87.3 3.3 %all-to-all-start.3 = ((f32[8,1,128,8]{2,3,1,0:T(8,128)}), f32[8,1,128,8]{2,3,1,0:T(8,128)S(1)}, u32[]{:S(2)}, u32[]{:S(2)}) async-start(f32[8,1,128,8]{2,3,1,0:T(8,128)} %bitcast.44), calls=%async_computation.3 | async-start | bytes 65536 | tf_op jit(solution)/shard_map/all_to_all | solution.py:144
  90.6 5.1 %fusion.16 = f32[8,8,128,128]{3,2,1,0:T(8,128)} fusion(bf16[8,128,8,128]{1,3,2,0:T(8,128)(2,1)S(1)} %bitcast.116, f32[8,8,128,128]{3,2,1,0:T(8,128)} %get-tuple-element.49, f32[8,8,128]{2,1,0:T(8,128)} %get-tuple-element.48), kind=kOutput, calls=%fused_computation.29 | convolution fusion | flops 271581184 | bytes 10518528 | tf_op jit(solution)/shard_map/gchqk,gckhd->gcqhd/dot_general | solution.py:42
  95.8 1.5 all-to-all-done.3
  97.3 4.7 %all-to-all-start.1 = ((f32[8,1,128,1024]{2,3,1,0:T(8,128)}), f32[8,1,128,1024]{2,3,1,0:T(8,128)}, u32[]{:S(2)}, u32[]{:S(2)}) async-start(f32[8,1,128,1024]{2,3,1,0:T(8,128)} %bitcast.110), calls=%async_computation.1 | async-start | bytes 8388608 | tf_op jit(solution)/shard_map/all_to_all | solution.py:142
  102.1 1.6 gather_fusion
  103.7 2.5 fusion.24
  106.4 4.6 %collective-permute-start = (bf16[2,128,1024]{2,1,0:T(8,128)(2,1)S(1)}, bf16[2,128,1024]{2,1,0:T(8,128)(2,1)}, u32[]{:S(2)}, u32[]{:S(2)}) collective-permute-start(bf16[2,128,1024]{2,1,0:T(8,128)(2,1)S(1)} %get-tuple-element.42), channel_id=1, source_target_pairs={{0,2},{2,4},{4,6},{6,8},{8,10},{10,12},{12,14},{1,3},{3,5},{5,7},{... | collective-permute-start | bytes 1572872 | tf_op jit(solution)/shard_map/ppermute | solution.py:20
  111.0 1.5 collective-permute-start.1
  112.5 0.1 pad.6.clone
  112.6 0.1 pad.23.clone
  112.7 0.1 reshape.630
  112.9 0.1 pad_add_fusion
  113.0 0.2 and_reduce_fusion
  113.3 0.1 copy.220
  113.4 0.8 bitcast_bitcast_fusion
  114.2 38.1 %collective-permute-done = bf16[2,128,1024]{2,1,0:T(8,128)(2,1)} collective-permute-done((bf16[2,128,1024]{2,1,0:T(8,128)(2,1)S(1)}, bf16[2,128,1024]{2,1,0:T(8,128)(2,1)}, u32[]{:S(2)}, u32[]{:S(2)}) %collective-permute-start) | collective-permute-done | bytes 524320 | tf_op jit(solution)/shard_map/ppermute | solution.py:20
  152.3 2.7 pad_maximum_fusion.1
  155.1 93.3 %all-reduce.3.cloned.1.call-done = bf16[2,2,128,1024]{3,2,0,1:T(8,128)(2,1)} async-done(((bf16[2,2,128,1024]{3,2,0,1:T(8,128)(2,1)}), bf16[2,2,128,1024]{3,2,0,1:T(8,128)(2,1)}) %all-reduce.3.cloned.1.call-update) | async-done | bytes 1048592 | tf_op jit(solution)/shard_map/psum | solution.py:101
  248.4 2.4 pad_maximum_fusion
  250.8 3.8 %gather_fusion.1 = bf16[10,2,128,1024]{3,2,1,0:T(8,128)(2,1)} fusion(bf16[2,6,128,1024]{3,2,1,0:T(8,128)(2,1)S(1)} %pad_maximum_fusion, s32[1024]{0:T(1024)S(1)} %pad_clamp_fusion.3), kind=kCustom, calls=%fused_computation.1 | custom fusion | bytes 10485800 | tf_op jit(solution)/shard_map/while/body/eval_jaxpr/jit(_take)/gather | solution.py:165
  254.6 8.0 %copy.182 = bf16[2,5,2,128,1024]{3,4,1,0,2:T(8,128)(2,1)} copy(bf16[2,5,2,128,1024]{4,3,2,1,0:T(8,128)(2,1)} %bitcast.109) | data formatting | bytes 10485760 | tf_op jit(solution)/shard_map/while/body/eval_jaxpr/jit(_take)/gather | solution.py:165
  262.6 3.1 %select_bitcast_fusion = bf16[2,2,5,128,1024]{3,4,2,1,0:T(8,128)(2,1)S(1)} fusion(bf16[2,5,2,128,1024]{3,4,1,0,2:T(8,128)(2,1)} %copy.182, pred[2,5]{1,0:T(4,128)(4,1)S(1)} %compare_and_fusion.4), kind=kLoop, calls=%fused_computation.13 | loop fusion | flops 2621440 | bytes 10485770 | tf_op jit(solution)/shard_map/while/body/eval_jaxpr/jit(_take)/select_n | solution.py:165
  265.7 0.4 fusion.47
  266.1 0.6 copy-done.5
  266.7 1.2 bitcast_reduce_fusion
  267.9 1.6 fusion.3
  269.5 3.2 %fusion.12 = f32[2,5,128,8,128]{2,4,3,1,0:T(8,128)} fusion(bf16[2,5,128,8,128]{2,4,3,1,0:T(8,128)(2,1)S(1)} %bitcast.114, bf16[2,5,8,128,128]{3,4,1,2,0:T(8,128)(2,1)S(1)} %get-tuple-element.26), kind=kOutput, calls=%fused_computation.27 | convolution fusion | flops 335544320 | bytes 10485760 | tf_op jit(solution)/shard_map/while/body/eval_jaxpr/gchqk,gckhd->gcqhd/dot_general | solution.py:42
  272.7 0.6 gather_fusion.5
  273.2 0.6 gather_fusion.6
  273.8 0.2 fusion.28
  274.1 2.9 gather_fusion.4
  277.0 3.2 %fusion.1 = f32[2,128,8,128]{1,3,2,0:T(8,128)S(1)} fusion(f32[2,3,128,8,128]{2,4,3,1,0:T(8,128)S(1)} %bitcast.113, f32[2,5,128,8,128]{2,4,3,1,0:T(8,128)} %fusion.12, f32[2,8,128,8]{2,3,1,0:T(8,128)S(1)} %copy.207), kind=kLoop, calls=%fused_computation.9 | loop fusion | flops 6029312 | bytes 9502720 | tf_op jit(solution)/shard_map/while/body/eval_jaxpr/reduce_sum | solution.py:56
  280.2 0.1 divide_convert_fusion
  280.3 0.3 copy.209
  280.7 0.9 copy.237
  281.6 8.8 %all-gather.2.cloned.1.call-done = bf16[256,2048]{1,0:T(8,128)(2,1)} async-done(((bf16[256,1024]{1,0:T(8,128)(2,1)}), bf16[256,2048]{1,0:T(8,128)(2,1)}) %all-gather.2.cloned.1.call-update) | async-done | bytes 1048592 | tf_op jit(solution)/shard_map/all_gather | solution.py:178
  290.4 4.6 %convolution_convert_fusion = bf16[256,1024]{1,0:T(8,128)(2,1)} fusion(bf16[256,2048]{1,0:T(8,128)(2,1)} %all-gather.2.cloned.1.call-done, bf16[2048,1024]{1,0:T(8,128)(2,1)} %param.10), kind=kOutput, calls=%fused_computation.36 | convolution fusion | flops 1074003968 | bytes 5767168 | tf_op jit(solution)/shard_map/dot_general | solution.py:177
  (53 shorter events, 0.7 us)
Async XLA Ops:
  10.1 9.5 %copy-start.1 = (bf16[256,1024]{1,0:T(8,128)(2,1)S(1)}, bf16[256,1024]{1,0:T(8,128)(2,1)}, u32[]{:S(2)}) copy-start(bf16[256,1024]{1,0:T(8,128)(2,1)} %param.9) | copy-start | bytes 1572868
  10.1 9.5 %copy-start.3 = (bf16[256,1024]{1,0:T(8,128)(2,1)S(1)}, bf16[256,1024]{1,0:T(8,128)(2,1)}, u32[]{:S(2)}) copy-start(bf16[256,1024]{1,0:T(8,128)(2,1)} %param.8) | copy-start | bytes 1572868
  11.7 55.7 %all-to-all-start = ((bf16[8,1,128,1024]{3,2,1,0:T(8,128)(2,1)}), bf16[8,1,128,1024]{3,2,1,0:T(8,128)(2,1)}, u32[]{:S(2)}, u32[]{:S(2)}) async-start(bf16[8,1,128,1024]{3,2,1,0:T(8,128)(2,1)} %fusion.18), calls=%async_computation | async-start | bytes 4194304 | tf_op jit(solution)/shard_map/all_to_all | solution.py:137
  77.0 10.3 %all-to-all-start.2 = ((f32[8,1,128,8]{2,3,1,0:T(8,128)}), f32[8,1,128,8]{2,3,1,0:T(8,128)S(1)}, u32[]{:S(2)}, u32[]{:S(2)}) async-start(f32[8,1,128,8]{2,3,1,0:T(8,128)} %bitcast.39), calls=%async_computation.2 | async-start | bytes 65536 | tf_op jit(solution)/shard_map/all_to_all | solution.py:143
  87.3 10.0 %all-to-all-start.3 = ((f32[8,1,128,8]{2,3,1,0:T(8,128)}), f32[8,1,128,8]{2,3,1,0:T(8,128)S(1)}, u32[]{:S(2)}, u32[]{:S(2)}) async-start(f32[8,1,128,8]{2,3,1,0:T(8,128)} %bitcast.44), calls=%async_computation.3 | async-start | bytes 65536 | tf_op jit(solution)/shard_map/all_to_all | solution.py:144
  97.3 4.8 %copy-start.6 = (s32[2]{0:T(128)S(1)}, s32[2]{0:T(128)}, u32[]{:S(2)}) copy-start(s32[2]{0:T(128)} %param.13) | copy-start | bytes 28
  97.3 176.8 %all-to-all-start.1 = ((f32[8,1,128,1024]{2,3,1,0:T(8,128)}), f32[8,1,128,1024]{2,3,1,0:T(8,128)}, u32[]{:S(2)}, u32[]{:S(2)}) async-start(f32[8,1,128,1024]{2,3,1,0:T(8,128)} %bitcast.110), calls=%async_computation.1 | async-start | bytes 8388608 | tf_op jit(solution)/shard_map/all_to_all | solution.py:142
  102.0 4.4 %copy-start.2 = (bf16[256,1024]{1,0:T(8,128)(2,1)S(1)}, bf16[256,1024]{1,0:T(8,128)(2,1)}, u32[]{:S(2)}) copy-start(bf16[256,1024]{1,0:T(8,128)(2,1)} %param.9) | copy-start | bytes 1572868
  102.0 4.3 %copy-start.4 = (bf16[256,1024]{1,0:T(8,128)(2,1)S(1)}, bf16[256,1024]{1,0:T(8,128)(2,1)}, u32[]{:S(2)}) copy-start(bf16[256,1024]{1,0:T(8,128)(2,1)} %param.8) | copy-start | bytes 1572868
  102.0 10.8 %copy-start.7 = (s32[2]{0:T(128)S(1)}, s32[2]{0:T(128)}, u32[]{:S(2)}) copy-start(s32[2]{0:T(128)} %param.12) | copy-start | bytes 28
  102.0 11.3 %copy-start = (bf16[256,1024]{1,0:T(8,128)(2,1)S(1)}, bf16[256,1024]{1,0:T(8,128)(2,1)}, u32[]{:S(2)}) copy-start(bf16[256,1024]{1,0:T(8,128)(2,1)} %param.7) | copy-start | bytes 1572868
  102.0 146.3 %all-reduce.3.cloned.1.call-start = ((), (), s32[]{:S(2)}) async-start(), calls=%async_computation.4 | async-start | bytes 2097152 | tf_op jit(solution)/shard_map/psum | solution.py:101
  106.3 184.1 %all-gather.2.cloned.1.call-start = ((), (), s32[]{:S(2)}) async-start(), calls=%async_computation.5 | async-start | bytes 1572864 | tf_op jit(solution)/shard_map/all_gather | solution.py:178
  106.4 45.9 %collective-permute-start = (bf16[2,128,1024]{2,1,0:T(8,128)(2,1)S(1)}, bf16[2,128,1024]{2,1,0:T(8,128)(2,1)}, u32[]{:S(2)}, u32[]{:S(2)}) collective-permute-start(bf16[2,128,1024]{2,1,0:T(8,128)(2,1)S(1)} %get-tuple-element.42), channel_id=1, source_target_pairs={{0,2},{2,4},{4,6},{6,8},{8,10},{10,12},{12,14},{1,3},{3,5},{5,7},{... | collective-permute-start | bytes 1572872 | tf_op jit(solution)/shard_map/ppermute | solution.py:20
  111.0 41.3 %collective-permute-start.1 = (bf16[2,128,1024]{2,1,0:T(8,128)(2,1)S(1)}, bf16[2,128,1024]{2,1,0:T(8,128)(2,1)}, u32[]{:S(2)}, u32[]{:S(2)}) collective-permute-start(bf16[2,128,1024]{2,1,0:T(8,128)(2,1)S(1)} %get-tuple-element.43), channel_id=1, source_target_pairs={{2,0},{4,2},{6,4},{8,6},{10,8},{12,10},{14,12},{3,1},{5,3},{7,5},{... | collective-permute-start | bytes 1572872 | tf_op jit(solution)/shard_map/ppermute | solution.py:23
  265.7 1.0 copy-start.5
Sparse Core Ops, SparseCore 0:
  106.4 141.9 all-reduce.2
  281.7 8.6 all-gather.1
where the time goes:
time: 303 us; the launch traced here: 302 us
  waiting for transfers between devices  180 us (59%)
  local copies, waits for them, and re-layouts  37.8 us (12%)
  other arithmetic  25.6 us (8%)
  starting transfers between devices  25.1 us (8%)
  matrix products  19.7 us (7%)
  between operations  13.8 us (5%)
    psum x1, waiting for transfers between devices, per_device(): global_pairs = lax.psum(global_terms.astype(jnp.bfloat16), 'ctx')  93.3 us
    ppermute x1, waiting for transfers between devices, with_halo(): lax.ppermute(lax.slice_in_dim(block, block.shape[dim] - width, None, axis...  38.1 us
    all_to_all x1, waiting for transfers between devices, per_device(): lax.all_to_all(outgoing, 'ctx', split_axis=0, concat_axis=0, tiled=True)  35 us
    gather x2, local copies, waits for them, and re-layouts, attend(): gathered = jnp.take(local_pool, index_group, axis=1)  11.8 us
    all_gather x1, waiting for transfers between devices, per_device(): lax.all_gather(attended, 'head', axis=1, tiled=True)  8.78 us
    dot_general x2, matrix products, block_partial(): jnp.einsum('gchqk,gckhd->gcqhd', weights.astype(jnp.bfloat16), value_head...  8.28 us
    all_to_all x1, starting transfers between devices, per_device(): lax.all_to_all(outgoing, 'ctx', split_axis=0, concat_axis=0, tiled=True)  7.31 us
    dot_general x2, matrix products, block_partial(): jnp.einsum('gqhd,gckhd->gchqk', query_heads, key_heads, preferred_element...  6.82 us
  transfers between devices with their start and end apart: 8, of which 6 were waited for; matrix products, arithmetic and copies ran while one was open for 18% of the time, Pallas kernels for 0%

commit v1 on v0

--- a/solution.py
+++ b/solution.py
@@ -98,7 +98,7 @@
     picked = jnp.take(own_blocks, global_slot, axis=1)
     owned_here = (global_owner == position)[None, :, None, None]
     global_terms = jnp.where(owned_here, picked.astype(jnp.float32), 0.0)
-    global_pairs = lax.psum(global_terms.astype(jnp.bfloat16), "ctx")
+    global_pairs = jnp.sum(lax.all_gather(global_terms.astype(jnp.bfloat16), "ctx"), axis=0)
     request_table = random_blocks.reshape(ctx_count, requests)
     owners = request_table // dev_blocks
     within = request_table % dev_blocks

time: 303 us -> 337 us (1.11)
  waiting for transfers between devices: 180 us -> 204 us
  other arithmetic: 25.6 us -> 31.3 us
  local copies, waits for them, and re-layouts: 37.8 us -> 43.3 us
    psum x1 -> x0, waiting for transfers between devices: 93.3 us -> none  [per_device(): global_pairs = lax.psum(global_terms.astype(jnp.bfloat16), 'ctx')]
    all_to_all x1, waiting for transfers between devices: 0.01 us -> 68 us  [per_device(): lax.all_to_all(part_out, 'ctx', split_axis=0, concat_axis=0, tiled=True)]
    all_to_all x1, waiting for transfers between devices: 35 us -> 64.5 us  [per_device(): lax.all_to_all(outgoing, 'ctx', split_axis=0, concat_axis=0, tiled=True)]
    all_gather x1, waiting for transfers between devices: 8.78 us -> 21.9 us  [per_device(): lax.all_gather(attended, 'head', axis=1, tiled=True)]
    reduce_sum x0 -> x1, other arithmetic: none -> 6.77 us  [per_device(): jnp.sum(lax.all_gather(global_terms.astype(jnp.bfloat16), 'ctx'), axis=0)]
    ppermute x1, waiting for transfers between devices: 38.1 us -> 44.2 us  [with_halo(): lax.ppermute(lax.slice_in_dim(block, block.shape[dim] - width, None, axis...]
  transfers between devices with their start and end apart: 8 -> 8, of which waited for: 6 -> 6; matrix products, arithmetic and copies ran while one was open for 18% -> 15% of each run, Pallas kernels for 0% -> 0%
where the time goes in v1:
time: 337 us; the launch traced here: 336 us
  waiting for transfers between devices  204 us (61%)
  local copies, waits for them, and re-layouts  43.3 us (13%)
  other arithmetic  31.3 us (9%)
  starting transfers between devices  25.8 us (8%)
  matrix products  18.1 us (5%)
  between operations  13.7 us (4%)
    all_to_all x1, waiting for transfers between devices, per_device(): lax.all_to_all(part_out, 'ctx', split_axis=0, concat_axis=0, tiled=True)  68 us
    all_to_all x1, waiting for transfers between devices, per_device(): lax.all_to_all(outgoing, 'ctx', split_axis=0, concat_axis=0, tiled=True)  64.5 us
    ppermute x1, waiting for transfers between devices, with_halo(): lax.ppermute(lax.slice_in_dim(block, block.shape[dim] - width, None, axis...  44.2 us
    all_gather x1, waiting for transfers between devices, per_device(): lax.all_gather(attended, 'head', axis=1, tiled=True)  21.9 us
    gather x2, local copies, waits for them, and re-layouts, attend(): gathered = jnp.take(local_pool, index_group, axis=1)  11.7 us
    all_to_all x1, starting transfers between devices, per_device(): lax.all_to_all(outgoing, 'ctx', split_axis=0, concat_axis=0, tiled=True)  7.31 us
    dot_general x2, matrix products, block_partial(): jnp.einsum('gqhd,gckhd->gchqk', query_heads, key_heads, preferred_element...  6.92 us
    reduce_sum x1, other arithmetic, per_device(): jnp.sum(lax.all_gather(global_terms.astype(jnp.bfloat16), 'ctx'), axis=0)  6.77 us
  transfers between devices with their start and end apart: 8, of which 6 were waited for; matrix products, arithmetic and copies ran while one was open for 15% of the time, Pallas kernels for 0%

profile of v1, /device:TPU:0, one launch (start us, length us, event | category | flops | bytes accessed | tf_op | source)
XLA Modules:
  0.0 336.1 jit_solution(4920446498483114145)
XLA Ops:
  6.5 0.7 compare_and_fusion.3
  7.2 1.3 pad_maximum_fusion.2
  8.5 0.6 gather_fusion
  9.2 0.3 select_convert_fusion
  9.5 1.1 copy.160
  10.7 0.1 copy.167
  10.8 0.1 copy.172
  10.9 0.1 copy.176
  11.0 0.2 convert_reduce_fusion
  11.3 0.2 compare_reduce_fusion
  11.5 0.2 add_reduce_fusion
  11.7 0.1 fusion.36
  11.8 2.0 gather_fusion.3
  13.8 3.2 fusion.18
  17.0 7.3 %all-to-all-start = ((bf16[8,1,128,1024]{3,2,1,0:T(8,128)(2,1)}), bf16[8,1,128,1024]{3,2,1,0:T(8,128)(2,1)}, u32[]{:S(2)}, u32[]{:S(2)}) async-start(bf16[8,1,128,1024]{3,2,1,0:T(8,128)(2,1)} %fusion.18), calls=%async_computation | async-start | bytes 4194304 | tf_op jit(solution)/shard_map/all_to_all | solution.py:137
  24.3 0.1 copy.177
  24.4 0.1 eq.96
  24.5 0.1 fusion.32
  24.7 0.1 reduce_sum.95
  24.9 2.8 gather_fusion.2
  27.6 2.7 bitcast_select_fusion
  30.3 2.5 fusion.47
  32.7 3.9 %copy.179 = bf16[1,8,1,128,1024]{3,4,1,2,0:T(8,128)(2,1)} copy(bf16[1,8,1,128,1024]{4,3,0,1,2:T(8,128)(2,1)} %get-tuple-element.40) | data formatting | bytes 4194304 | tf_op jit(solution)/shard_map/slice | solution.py:141
  36.7 3.9 %copy.178 = bf16[1,8,1,128,1024]{3,4,1,2,0:T(8,128)(2,1)} copy(bf16[1,8,1,128,1024]{4,3,0,1,2:T(8,128)(2,1)} %get-tuple-element.41) | data formatting | bytes 4194304 | tf_op jit(solution)/shard_map/slice | solution.py:141
  40.6 64.5 %all-to-all-done = bf16[8,1,128,1024]{3,2,1,0:T(8,128)(2,1)} async-done(((bf16[8,1,128,1024]{3,2,1,0:T(8,128)(2,1)}), bf16[8,1,128,1024]{3,2,1,0:T(8,128)(2,1)}, u32[]{:S(2)}, u32[]{:S(2)}) %all-to-all-start) | async-done | bytes 2097184 | tf_op jit(solution)/shard_map/all_to_all | solution.py:137
  105.1 4.0 %copy.181 = bf16[8,1,128,1024]{2,3,0,1:T(8,128)(2,1)} copy(bf16[8,1,128,1024]{3,2,1,0:T(8,128)(2,1)} %all-to-all-done) | data formatting | bytes 4194304 | tf_op jit(solution)/shard_map/all_to_all | solution.py:137
  109.1 5.7 %bitcast_reduce_fusion.1 = (f32[8,8,128]{2,1,0:T(8,128)}, f32[8,8,128,128]{3,2,1,0:T(8,128)}) fusion(bf16[8,128,8,128]{1,3,2,0:T(8,128)(2,1)} %bitcast.122, bf16[8,128,8,128]{1,3,2,0:T(8,128)(2,1)} %bitcast.123), kind=kOutput, calls=%fused_computation.18 | convolution fusion | flops 270524416 | bytes 8421376 | tf_op jit(solution)/shard_map/gqhd,gckhd->gchqk/dot_general | solution.py:36
  114.8 3.4 %all-to-all-start.2 = ((f32[8,1,128,8]{2,3,1,0:T(8,128)}), f32[8,1,128,8]{2,3,1,0:T(8,128)S(1)}, u32[]{:S(2)}, u32[]{:S(2)}) async-start(f32[8,1,128,8]{2,3,1,0:T(8,128)} %bitcast.40), calls=%async_computation.2 | async-start | bytes 65536 | tf_op jit(solution)/shard_map/all_to_all | solution.py:143
  118.3 3.7 %fusion.6 = f32[8,8,128]{2,1,0:T(8,128)} fusion(f32[8,8,128,128]{3,2,1,0:T(8,128)} %get-tuple-element.49, f32[8,8,128]{2,1,0:T(8,128)} %get-tuple-element.48), kind=kLoop, calls=%fused_computation.20 | loop fusion | flops 3137536 | bytes 4259840 | tf_op jit(solution)/shard_map/reduce_sum | solution.py:41
  122.0 3.6 %all-to-all-done.2 = f32[8,1,128,8]{2,3,1,0:T(8,128)S(1)} async-done(((f32[8,1,128,8]{2,3,1,0:T(8,128)}), f32[8,1,128,8]{2,3,1,0:T(8,128)S(1)}, u32[]{:S(2)}, u32[]{:S(2)}) %all-to-all-start.2) | async-done | bytes 32800 | tf_op jit(solution)/shard_map/all_to_all | solution.py:143
  125.6 4.3 %all-to-all-start.3 = ((f32[8,1,128,8]{2,3,1,0:T(8,128)}), f32[8,1,128,8]{2,3,1,0:T(8,128)S(1)}, u32[]{:S(2)}, u32[]{:S(2)}) async-start(f32[8,1,128,8]{2,3,1,0:T(8,128)} %bitcast.45), calls=%async_computation.3 | async-start | bytes 65536 | tf_op jit(solution)/shard_map/all_to_all | solution.py:144
  129.9 5.8 %fusion.16 = f32[8,8,128,128]{3,2,1,0:T(8,128)} fusion(bf16[8,128,8,128]{1,3,2,0:T(8,128)(2,1)} %bitcast.120, f32[8,8,128,128]{3,2,1,0:T(8,128)} %get-tuple-element.49, f32[8,8,128]{2,1,0:T(8,128)} %get-tuple-element.48), kind=kOutput, calls=%fused_computation.29 | convolution fusion | flops 271581184 | bytes 10518528 | tf_op jit(solution)/shard_map/gchqk,gckhd->gcqhd/dot_general | solution.py:42
  135.7 1.6 all-to-all-done.3
  137.3 4.7 %all-to-all-start.1 = ((f32[8,1,128,1024]{2,3,1,0:T(8,128)}), f32[8,1,128,1024]{2,3,1,0:T(8,128)}, u32[]{:S(2)}, u32[]{:S(2)}) async-start(f32[8,1,128,1024]{2,3,1,0:T(8,128)} %bitcast.114), calls=%async_computation.1 | async-start | bytes 8388608 | tf_op jit(solution)/shard_map/all_to_all | solution.py:142
  142.1 4.6 %collective-permute-start = (bf16[2,128,1024]{2,1,0:T(8,128)(2,1)S(1)}, bf16[2,128,1024]{2,1,0:T(8,128)(2,1)}, u32[]{:S(2)}, u32[]{:S(2)}) collective-permute-start(bf16[2,128,1024]{2,1,0:T(8,128)(2,1)S(1)} %get-tuple-element.42), channel_id=1, source_target_pairs={{0,2},{2,4},{4,6},{6,8},{8,10},{10,12},{12,14},{1,3},{3,5},{5,7},{... | collective-permute-start | bytes 1572872 | tf_op jit(solution)/shard_map/ppermute | solution.py:20
  146.7 1.5 collective-permute-start.1
  148.4 0.1 reshape.646
  148.7 0.2 and_reduce_fusion
  149.0 0.1 copy.202
  149.1 0.8 bitcast_bitcast_fusion
  149.9 44.2 %collective-permute-done = bf16[2,128,1024]{2,1,0:T(8,128)(2,1)} collective-permute-done((bf16[2,128,1024]{2,1,0:T(8,128)(2,1)S(1)}, bf16[2,128,1024]{2,1,0:T(8,128)(2,1)}, u32[]{:S(2)}, u32[]{:S(2)}) %collective-permute-start) | collective-permute-done | bytes 524320 | tf_op jit(solution)/shard_map/ppermute | solution.py:20
  194.1 2.7 pad_maximum_fusion.1
  196.8 0.6 gather_fusion.5
  197.4 0.6 gather_fusion.6
  198.0 68.0 %all-to-all-done.1 = f32[8,1,128,1024]{2,3,1,0:T(8,128)} async-done(((f32[8,1,128,1024]{2,3,1,0:T(8,128)}), f32[8,1,128,1024]{2,3,1,0:T(8,128)}, u32[]{:S(2)}, u32[]{:S(2)}) %all-to-all-start.1) | async-done | bytes 4194336 | tf_op jit(solution)/shard_map/all_to_all | solution.py:142
  266.0 4.6 %gather_fusion.4 = f32[6,128,1024]{1,2,0:T(8,128)} fusion(f32[8,128,1024]{1,2,0:T(8,128)} %bitcast.35, s32[1024]{0:T(1024)S(1)} %pad_clamp_fusion), kind=kCustom, calls=%fused_computation.4 | custom fusion | bytes 6291480 | tf_op jit(solution)/shard_map/gather | solution.py:146
  270.6 6.8 %reduce_sum.91 = bf16[2,2,128,1024]{3,2,1,0:T(8,128)(2,1)} reduce(bf16[8,2,2,128,1024]{4,3,2,1,0:T(8,128)(2,1)} %all-gather.3.cloned.1.call-done, bf16[]{:T(256)} %constant.162.clone.1), dimensions={0}, to_apply=%region_0.1 | reduce | flops 3670016 | bytes 9437186 | tf_op jit(solution)/shard_map/reduce_sum | solution.py:101
  277.3 2.2 pad_maximum_fusion
  279.5 3.8 %gather_fusion.1 = bf16[10,2,128,1024]{3,2,1,0:T(8,128)(2,1)} fusion(bf16[2,6,128,1024]{3,2,1,0:T(8,128)(2,1)S(1)} %pad_maximum_fusion, s32[1024]{0:T(1024)S(1)} %pad_clamp_fusion.3), kind=kCustom, calls=%fused_computation.1 | custom fusion | bytes 10485800 | tf_op jit(solution)/shard_map/while/body/eval_jaxpr/jit(_take)/gather | solution.py:165
  283.4 7.9 %copy.163 = bf16[2,5,2,128,1024]{3,4,1,0,2:T(8,128)(2,1)} copy(bf16[2,5,2,128,1024]{4,3,2,1,0:T(8,128)(2,1)} %bitcast.113) | data formatting | bytes 10485760 | tf_op jit(solution)/shard_map/while/body/eval_jaxpr/jit(_take)/gather | solution.py:165
  291.3 3.1 select_bitcast_fusion
  294.3 0.5 fusion.46
  294.8 0.6 copy-done.4
  295.4 1.2 bitcast_reduce_fusion
  296.5 1.5 fusion.3
  298.1 0.2 fusion.27
  298.4 0.8 fusion.12
  299.2 1.0 copy-done.1
  300.2 1.3 fusion.1
  301.5 0.1 divide_convert_fusion
  301.6 0.3 copy.190
  301.9 0.9 copy.217
  302.9 21.9 %all-gather.5.cloned.1.call-done = bf16[256,2048]{1,0:T(8,128)(2,1)} async-done(((bf16[256,1024]{1,0:T(8,128)(2,1)}), bf16[256,2048]{1,0:T(8,128)(2,1)}) %all-gather.5.cloned.1.call-update) | async-done | bytes 1048592 | tf_op jit(solution)/shard_map/all_gather | solution.py:178
  324.7 4.6 %convolution_convert_fusion = bf16[256,1024]{1,0:T(8,128)(2,1)} fusion(bf16[256,2048]{1,0:T(8,128)(2,1)} %all-gather.5.cloned.1.call-done, bf16[2048,1024]{1,0:T(8,128)(2,1)} %param.10), kind=kOutput, calls=%fused_computation.36 | convolution fusion | flops 1074003968 | bytes 5767168 | tf_op jit(solution)/shard_map/dot_general | solution.py:177
  (54 shorter events, 0.9 us)
Async XLA Ops:
  6.5 264.0 %all-gather.3.cloned.1.call-start = ((), (), s32[]{:S(2)}) async-start(), calls=%async_computation.4 | async-start | bytes 9437184 | tf_op jit(solution)/shard_map/all_gather | solution.py:101
  8.5 2.1 copy-start.5
  8.5 3.3 copy-start
  17.0 88.1 %all-to-all-start = ((bf16[8,1,128,1024]{3,2,1,0:T(8,128)(2,1)}), bf16[8,1,128,1024]{3,2,1,0:T(8,128)(2,1)}, u32[]{:S(2)}, u32[]{:S(2)}) async-start(bf16[8,1,128,1024]{3,2,1,0:T(8,128)(2,1)} %fusion.18), calls=%async_computation | async-start | bytes 4194304 | tf_op jit(solution)/shard_map/all_to_all | solution.py:137
  114.8 10.7 %all-to-all-start.2 = ((f32[8,1,128,8]{2,3,1,0:T(8,128)}), f32[8,1,128,8]{2,3,1,0:T(8,128)S(1)}, u32[]{:S(2)}, u32[]{:S(2)}) async-start(f32[8,1,128,8]{2,3,1,0:T(8,128)} %bitcast.40), calls=%async_computation.2 | async-start | bytes 65536 | tf_op jit(solution)/shard_map/all_to_all | solution.py:143
  125.6 11.7 %all-to-all-start.3 = ((f32[8,1,128,8]{2,3,1,0:T(8,128)}), f32[8,1,128,8]{2,3,1,0:T(8,128)S(1)}, u32[]{:S(2)}, u32[]{:S(2)}) async-start(f32[8,1,128,8]{2,3,1,0:T(8,128)} %bitcast.45), calls=%async_computation.3 | async-start | bytes 65536 | tf_op jit(solution)/shard_map/all_to_all | solution.py:144
  137.2 4.8 %copy-start.2 = (bf16[256,1024]{1,0:T(8,128)(2,1)S(1)}, bf16[256,1024]{1,0:T(8,128)(2,1)}, u32[]{:S(2)}) copy-start(bf16[256,1024]{1,0:T(8,128)(2,1)} %param.9) | copy-start | bytes 1572868
  137.3 4.8 %copy-start.3 = (bf16[256,1024]{1,0:T(8,128)(2,1)S(1)}, bf16[256,1024]{1,0:T(8,128)(2,1)}, u32[]{:S(2)}) copy-start(bf16[256,1024]{1,0:T(8,128)(2,1)} %param.8) | copy-start | bytes 1572868
  137.3 10.9 %copy-start.6 = (s32[2]{0:T(128)S(1)}, s32[2]{0:T(128)}, u32[]{:S(2)}) copy-start(s32[2]{0:T(128)} %param.13) | copy-start | bytes 28
  137.3 11.2 %copy-start.7 = (s32[2]{0:T(128)S(1)}, s32[2]{0:T(128)}, u32[]{:S(2)}) copy-start(s32[2]{0:T(128)} %param.12) | copy-start | bytes 28
  137.3 128.7 %all-to-all-start.1 = ((f32[8,1,128,1024]{2,3,1,0:T(8,128)}), f32[8,1,128,1024]{2,3,1,0:T(8,128)}, u32[]{:S(2)}, u32[]{:S(2)}) async-start(f32[8,1,128,1024]{2,3,1,0:T(8,128)} %bitcast.114), calls=%async_computation.1 | async-start | bytes 8388608 | tf_op jit(solution)/shard_map/all_to_all | solution.py:142
  142.0 182.8 %all-gather.5.cloned.1.call-start = ((), (), s32[]{:S(2)}) async-start(), calls=%async_computation.5 | async-start | bytes 1572864 | tf_op jit(solution)/shard_map/all_gather | solution.py:178
  142.1 52.0 %collective-permute-start = (bf16[2,128,1024]{2,1,0:T(8,128)(2,1)S(1)}, bf16[2,128,1024]{2,1,0:T(8,128)(2,1)}, u32[]{:S(2)}, u32[]{:S(2)}) collective-permute-start(bf16[2,128,1024]{2,1,0:T(8,128)(2,1)S(1)} %get-tuple-element.42), channel_id=1, source_target_pairs={{0,2},{2,4},{4,6},{6,8},{8,10},{10,12},{12,14},{1,3},{3,5},{5,7},{... | collective-permute-start | bytes 1572872 | tf_op jit(solution)/shard_map/ppermute | solution.py:20
  146.7 47.4 %collective-permute-start.1 = (bf16[2,128,1024]{2,1,0:T(8,128)(2,1)S(1)}, bf16[2,128,1024]{2,1,0:T(8,128)(2,1)}, u32[]{:S(2)}, u32[]{:S(2)}) collective-permute-start(bf16[2,128,1024]{2,1,0:T(8,128)(2,1)S(1)} %get-tuple-element.43), channel_id=1, source_target_pairs={{2,0},{4,2},{6,4},{8,6},{10,8},{12,10},{14,12},{3,1},{5,3},{7,5},{... | collective-permute-start | bytes 1572872 | tf_op jit(solution)/shard_map/ppermute | solution.py:23
  294.3 1.0 copy-start.4
  298.3 1.9 copy-start.1
Sparse Core Ops, SparseCore 0:
  10.8 234.3 all-gather.2
  303.0 21.7 all-gather.4
